TPU v7x, 128 devices: a whole 4x4x4 slice. The times are simulated.
128 devices in a mesh: dp: 16 (over y, x), head: 8 (over z, core).
Axes of the slice: x: 4, y: 4, z: 4, core: 2. Of those that a mesh axis runs over, the one named last changes fastest.
Arguments:
- slot_token_ids: int32 [128, 512], P('dp'), may hold values from 0 to 50264
- lengths: int32 [128], P('dp'), may hold values from 64 to 512, as said below
- labels: int32 [128], P('dp'), may hold values from 0 to 2
- optimizer_step_count: int32 [], replicated, may hold values from 2 to 20
- token_embedding_table: bfloat16 [50304, 1024], P('dp', 'head'), may hold values from -6 to 6
- positions: bfloat16 [512, 1024], replicated, may hold values from -4 to 4
- query_key_value_weight: bfloat16 [3, 1024, 1024], P(None, None, 'head'), may hold values from -0.1875 to 0.1875
- attention_output_weight: bfloat16 [1024, 1024], P('head'), may hold values from -0.8 to 0.8
- feedforward_input_weight: bfloat16 [1024, 4096], P(None, 'head'), may hold values from -0.1875 to 0.1875
- feedforward_output_weight: bfloat16 [4096, 1024], P('head'), may hold values from -0.09375 to 0.09375
- layer_norm_gains: float32 [3, 1024], replicated, may hold values from 0.5 to 1.5
- layer_norm_biases: float32 [3, 1024], replicated, may hold values from -2 to 2
- classifier: bfloat16 [3, 1024], replicated, may hold values from -0.75 to 0.75
- adapter_down_maps: float32 [2, 1024, 16], replicated, may hold values from -0.1875 to 0.1875
- adapter_up_maps: float32 [2, 16, 1024], P(None, None, 'head'), may hold values from -1.5 to 1.5
- down_first_moment: float32 [2, 1024, 16], P(None, 'dp'), may hold values from -0.0078125 to 0.0078125
- down_second_moment: float32 [2, 1024, 16], P(None, 'dp'), may hold values from 2.1972657e-08 to 9.1552735e-08
- up_first_moment: float32 [2, 16, 1024], P(None, None, ('head', 'dp')), may hold values from -0.0078125 to 0.0078125
- up_second_moment: float32 [2, 16, 1024], P(None, None, ('head', 'dp')), may hold values from 2.1972657e-08 to 9.1552735e-08
- down_privacy_noise: float32 [2, 1024, 16], P(None, 'dp'), may hold values from -6 to 6
- up_privacy_noise: float32 [2, 16, 1024], P(None, None, ('head', 'dp')), may hold values from -6 to 6
Outputs:
- loss: float32 [], replicated
- example_norms: float32 [128], P(('dp', 'head'))
- a_moment1: float32 [2, 1024, 16], P(None, 'dp')
- a_moment2: float32 [2, 1024, 16], P(None, 'dp')
- a_weight: float32 [2, 1024, 16], P(None, 'dp')
- b_moment1: float32 [2, 16, 1024], P(None, None, ('head', 'dp'))
- b_moment2: float32 [2, 16, 1024], P(None, None, ('head', 'dp'))
- b_weight: float32 [2, 16, 1024], P(None, None, ('head', 'dp'))
- lamb_norms: float32 [4, 2], replicated
Inputs may be any that keep to these rules, and one draw needn't show every extreme that they name: `lengths`: valid tokens of each example; some example has exactly 512.
All inputs are finite; a program needn't handle non-finite values.
Results may differ from a plain program's by a relative error of at most 0.0059.
Values may be sent and summed in bfloat16 or wider, within the bound.
No kernel may reach another device: no remote copies, remote signals or barrier semaphores. Data moves between devices by JAX's collectives and lax.ppermute only.
A program may use at most 256 MiB of HBM per device.

v0:
```python
import jax
import jax.numpy as jnp
from jax import lax
from jax.sharding import PartitionSpec as P

HDIM = 64
MICRO = 4
precise = lax.Precision.HIGHEST
adapter_scale = 2.0
clip_bound = 1.0
noise_mult = 0.6
smooth_rate = 0.1
beta_one = 0.9
beta_two = 0.999
adam_eps = 1e-06
decay_rate = 0.01
learn_rate = 0.25
norm_eps = 1e-05
contract_last = (((1,), (1,)), ((), ()))


def gelu_exact(inputs):
    return jax.nn.gelu(inputs, approximate=False)


def norm_rows(inputs, gain, bias):
    centre = inputs - jnp.mean(inputs, -1, keepdims=True)
    inv_std = lax.rsqrt(jnp.mean(centre * centre, -1, keepdims=True) + norm_eps)
    return (centre * inv_std * gain + bias, inv_std)


def norm_back(grad, normed, inv_std, gain, bias):
    x_hat = (normed - bias) / gain
    scaled = grad * gain
    return inv_std * (
        scaled
        - jnp.mean(scaled, -1, keepdims=True)
        - x_hat * jnp.mean(scaled * x_hat, -1, keepdims=True)
    )


def branch_add(partial_out, resid, gain, bias):
    total = lax.psum(partial_out, "head")
    return norm_rows(resid + total, gain, bias)


def masked_scores(query_h, key_h, valid_mask):
    scores = jnp.einsum(
        "eqhd,ekhd->ehqk", query_h, key_h, preferred_element_type=jnp.float32
    ) * HDIM ** (-0.5)
    return jnp.where(valid_mask[:, None, None, :], scores, -1e30)


def layer_forward(
    hidden_initial, valid_mask, length_float, class_label, frozen_params, adapter_reduced
):
    w_qkv, w_o, w_in, w_out, gains, biases, class_w = frozen_params
    down_pair, up_reduced = adapter_reduced
    example_count, sequence_length = valid_mask.shape
    width = hidden_initial.shape[1]
    local_w = w_o.shape[0]
    adapter_width = up_reduced.shape[1]
    shape4 = (example_count, sequence_length, local_w // HDIM, HDIM)
    hidden_reduced = hidden_initial.astype(jnp.bfloat16)
    adapter_activation = jnp.dot(
        hidden_reduced, down_pair, preferred_element_type=jnp.float32
    ).astype(jnp.bfloat16)
    query_low = (
        (
            jnp.dot(hidden_reduced, w_qkv[0], preferred_element_type=jnp.float32)
            + adapter_scale
            * jnp.dot(
                adapter_activation[:, :adapter_width],
                up_reduced[0],
                preferred_element_type=jnp.float32,
            )
        )
        .astype(jnp.bfloat16)
        .reshape(shape4)
    )
    key_low = (
        jnp.dot(hidden_reduced, w_qkv[1], preferred_element_type=jnp.float32)
        .astype(jnp.bfloat16)
        .reshape(shape4)
    )
    value_low = (
        (
            jnp.dot(hidden_reduced, w_qkv[2], preferred_element_type=jnp.float32)
            + adapter_scale
            * jnp.dot(
                adapter_activation[:, adapter_width:],
                up_reduced[1],
                preferred_element_type=jnp.float32,
            )
        )
        .astype(jnp.bfloat16)
        .reshape(shape4)
    )
    scores = masked_scores(query_low, key_low, valid_mask)
    row_top = jnp.max(scores, -1, keepdims=True)
    log_total = row_top + jnp.log(jnp.sum(jnp.exp(scores - row_top), -1, keepdims=True))
    attn_prob = jnp.exp(scores - log_total)
    context = (
        jnp.einsum(
            "ehqk,ekhd->eqhd",
            attn_prob.astype(jnp.bfloat16),
            value_low,
            preferred_element_type=jnp.float32,
        )
        .astype(jnp.bfloat16)
        .reshape(-1, local_w)
    )
    hidden_one, std_one = branch_add(
        jnp.dot(context, w_o, preferred_element_type=jnp.float32),
        hidden_initial,
        gains[1],
        biases[1],
    )
    ffn_pre = jnp.dot(hidden_one.astype(jnp.bfloat16), w_in, preferred_element_type=jnp.float32)
    ffn_part = jnp.dot(
        gelu_exact(ffn_pre).astype(jnp.bfloat16), w_out, preferred_element_type=jnp.float32
    )
    hidden_two, std_two = branch_add(ffn_part, hidden_one, gains[2], biases[2])
    valid_f = valid_mask.astype(jnp.float32)
    pooled = (
        jnp.sum(hidden_two.reshape(example_count, sequence_length, width) * valid_f[..., None], 1)
        / length_float[:, None]
    )
    logits = lax.dot_general(
        pooled.astype(jnp.bfloat16), class_w, contract_last, preferred_element_type=jnp.float32
    )
    log_prob = jax.nn.log_softmax(logits, -1)
    target = (1.0 - smooth_rate) * jax.nn.one_hot(
        class_label, class_w.shape[0], dtype=jnp.float32
    ) + smooth_rate / class_w.shape[0]
    losses = -jnp.sum(target * log_prob, -1)
    d_logit = jnp.exp(log_prob) - target
    d_pooled = jnp.dot(d_logit, class_w.astype(jnp.float32), precision=precise)
    d_two = (d_pooled[:, None, :] * (valid_f / length_float[:, None])[..., None]).reshape(-1, width)
    d_sum_two = norm_back(d_two, hidden_two, std_two, gains[2], biases[2])
    grad_act = lax.dot_general(
        d_sum_two.astype(jnp.bfloat16), w_out, contract_last, preferred_element_type=jnp.float32
    )
    d_pre = jax.vjp(gelu_exact, ffn_pre)[1](grad_act)[0].astype(jnp.bfloat16)
    back_part = lax.dot_general(d_pre, w_in, contract_last, preferred_element_type=jnp.float32)
    d_one = d_sum_two + lax.psum(back_part, "head")
    d_attn = norm_back(d_one, hidden_one, std_one, gains[1], biases[1]).astype(jnp.bfloat16)
    d_context = (
        lax.dot_general(d_attn, w_o, contract_last, preferred_element_type=jnp.float32)
        .astype(jnp.bfloat16)
        .reshape(shape4)
    )
    attn_prob = jnp.exp(masked_scores(query_low, key_low, valid_mask) - log_total)
    d_value = jnp.einsum(
        "ehqk,eqhd->ekhd",
        attn_prob.astype(jnp.bfloat16),
        d_context,
        preferred_element_type=jnp.float32,
    ).astype(jnp.bfloat16)
    d_prob = jnp.einsum("eqhd,ekhd->ehqk", d_context, value_low, preferred_element_type=jnp.float32)
    d_score = (attn_prob * (d_prob - jnp.sum(attn_prob * d_prob, -1, keepdims=True))).astype(
        jnp.bfloat16
    )
    d_query = (
        jnp.einsum("ehqk,ekhd->eqhd", d_score, key_low, preferred_element_type=jnp.float32)
        * HDIM ** (-0.5)
    ).astype(jnp.bfloat16)
    dq_rows = d_query.reshape(-1, local_w)
    dv_rows = d_value.reshape(-1, local_w)
    example_activation = adapter_activation.reshape(
        example_count, sequence_length, 2 * adapter_width
    )
    up_gradient = adapter_scale * jnp.stack(
        [
            jnp.einsum(
                "elr,eld->erd",
                example_activation[..., :adapter_width],
                dq_rows.reshape(example_count, sequence_length, local_w),
                preferred_element_type=jnp.float32,
            ),
            jnp.einsum(
                "elr,eld->erd",
                example_activation[..., adapter_width:],
                dv_rows.reshape(example_count, sequence_length, local_w),
                preferred_element_type=jnp.float32,
            ),
        ],
        1,
    )
    inner_portion = adapter_scale * jnp.concatenate(
        [
            lax.dot_general(
                dq_rows, up_reduced[0], contract_last, preferred_element_type=jnp.float32
            ),
            lax.dot_general(
                dv_rows, up_reduced[1], contract_last, preferred_element_type=jnp.float32
            ),
        ],
        1,
    )
    inner_full = lax.psum(inner_portion, "head")
    inner_sum = inner_full.astype(jnp.bfloat16)
    grad_both = jnp.einsum(
        "eld,elr->edr",
        hidden_reduced.reshape(example_count, sequence_length, width),
        inner_sum.reshape(example_count, sequence_length, 2 * adapter_width),
        preferred_element_type=jnp.float32,
    )
    down_gradient = jnp.stack([grad_both[..., :adapter_width], grad_both[..., adapter_width:]], 1)
    return (losses, down_gradient, up_gradient)


def apply_blocks(hidden_rows, lengths, labels, frozen_params, adapter_reduced, encoder_block):
    example_count, sequence_length, width = hidden_rows.shape
    valid_all = jnp.arange(sequence_length)[None, :] < lengths[:, None]
    loss_list, down_list, up_list = ([], [], [])
    for block_idx in range(example_count // encoder_block):
        first_ex = block_idx * encoder_block
        last_ex = first_ex + encoder_block
        losses, down_gradient, up_gradient = layer_forward(
            hidden_rows[first_ex:last_ex].reshape(-1, width),
            valid_all[first_ex:last_ex],
            lengths[first_ex:last_ex].astype(jnp.float32),
            labels[first_ex:last_ex],
            frozen_params,
            adapter_reduced,
        )
        loss_list.append(losses)
        down_list.append(down_gradient)
        up_list.append(up_gradient)
    return (
        jnp.concatenate(loss_list, 0),
        jnp.concatenate(down_list, 0),
        jnp.concatenate(up_list, 0),
    )


def lamb_direction(weight, grad, first, second, step_number):
    first_new = beta_one * first + (1.0 - beta_one) * grad
    second_new = beta_two * second + (1.0 - beta_two) * grad * grad
    direction = (
        first_new
        / (1.0 - jnp.power(beta_one, step_number))
        / (jnp.sqrt(second_new / (1.0 - jnp.power(beta_two, step_number))) + adam_eps)
        + decay_rate * weight
    )
    return (first_new, second_new, direction)


def per_device(
    slot_token_ids,
    lengths,
    labels,
    optimizer_step_count,
    token_embedding_table,
    positions,
    query_key_value_weight,
    attention_output_weight,
    feedforward_input_weight,
    feedforward_output_weight,
    layer_norm_gains,
    layer_norm_biases,
    classifier,
    adapter_down_maps,
    adapter_up_maps,
    down_first_moment,
    down_second_moment,
    up_first_moment,
    up_second_moment,
    down_privacy_noise,
    up_privacy_noise,
):
    n_head = lax.axis_size("head")
    dataset_size = lax.axis_size("dp")
    ex_dev, sequence_length = slot_token_ids.shape
    width = positions.shape[1]
    every_ids = lax.all_gather(slot_token_ids, "dp", axis=0, tiled=True).reshape(-1)
    vocab_local = token_embedding_table.shape[0]
    offset = lax.axis_index("dp") * vocab_local
    ids_here = every_ids - offset
    inside = (ids_here >= 0) & (ids_here < vocab_local)
    picked = jnp.take(token_embedding_table, jnp.clip(ids_here, 0, vocab_local - 1), axis=0)
    columns = lax.psum_scatter(
        jnp.where(inside[:, None], picked.astype(jnp.float32), 0.0).astype(jnp.bfloat16),
        "dp",
        scatter_dimension=0,
        tiled=True,
    )
    pos_f = positions.astype(jnp.float32)[None]
    down_reduced = adapter_down_maps.astype(jnp.bfloat16)
    down_pair = jnp.concatenate([down_reduced[0], down_reduced[1]], 1)
    micro_examples = ex_dev // MICRO
    own_share = ex_dev // n_head
    tokens = lax.all_gather(columns, "head", axis=1, tiled=True)
    hidden_all, unused_std = norm_rows(
        tokens.astype(jnp.float32).reshape(ex_dev, sequence_length, width) + pos_f,
        layer_norm_gains[0],
        layer_norm_biases[0],
    )
    frozen_params = (
        query_key_value_weight,
        attention_output_weight,
        feedforward_input_weight,
        feedforward_output_weight,
        layer_norm_gains,
        layer_norm_biases,
        classifier,
    )
    losses, grads_down, grads_up = apply_blocks(
        hidden_all,
        lengths,
        labels,
        frozen_params,
        (down_pair, adapter_up_maps.astype(jnp.bfloat16)),
        micro_examples,
    )
    part_sums = jnp.sum(grads_down * grads_down, (1, 2, 3)) / n_head + jnp.sum(
        grads_up * grads_up, (1, 2, 3)
    )
    arrived = lax.all_to_all(
        part_sums.reshape(n_head, own_share), "head", split_axis=0, concat_axis=0, tiled=True
    )
    example_norms = jnp.sqrt(jnp.sum(arrived, 0))
    own_factor = clip_bound / jnp.maximum(example_norms, clip_bound)
    factors = lax.all_gather(own_factor, "head", axis=0, tiled=True)
    sum_down = jnp.einsum("e,eabc->abc", factors, grads_down, precision=precise)
    sum_up = jnp.einsum("e,eabc->abc", factors, grads_up, precision=precise)
    loss_part = jnp.sum(losses) / n_head
    red_down, red_up = (
        lax.psum_scatter(sum_down, "dp", scatter_dimension=1, tiled=True),
        lax.psum_scatter(sum_up, "dp", scatter_dimension=2, tiled=True),
    )
    examples = ex_dev * dataset_size
    down_gradient = (red_down + noise_mult * clip_bound * down_privacy_noise) / examples
    up_gradient = (red_up + noise_mult * clip_bound * up_privacy_noise) / examples
    step_number = optimizer_step_count.astype(jnp.float32)
    down_rows = adapter_down_maps.shape[1] // dataset_size
    down_weight = lax.dynamic_slice_in_dim(
        adapter_down_maps, lax.axis_index("dp") * down_rows, down_rows, 1
    )
    up_columns = adapter_up_maps.shape[2] // dataset_size
    up_weight = lax.dynamic_slice_in_dim(
        adapter_up_maps, lax.axis_index("dp") * up_columns, up_columns, 2
    )
    down_momentum, down_velocity, dir_down = lamb_direction(
        down_weight, down_gradient, down_first_moment, down_second_moment, step_number
    )
    up_momentum, up_velocity, dir_up = lamb_direction(
        up_weight, up_gradient, up_first_moment, up_second_moment, step_number
    )
    sq_down = (
        jnp.stack(
            [jnp.sum(down_weight * down_weight, (1, 2)), jnp.sum(dir_down * dir_down, (1, 2))], 1
        )
        / n_head
    )
    sq_up = jnp.stack([jnp.sum(up_weight * up_weight, (1, 2)), jnp.sum(dir_up * dir_up, (1, 2))], 1)
    total_down, total_up, loss_sum = lax.psum((sq_down, sq_up, loss_part), ("dp", "head"))
    norm_table = jnp.sqrt(jnp.concatenate([total_down, total_up], 0))
    updated_down = (
        down_weight - learn_rate * (norm_table[:2, 0] / norm_table[:2, 1])[:, None, None] * dir_down
    )
    updated_up = (
        up_weight - learn_rate * (norm_table[2:, 0] / norm_table[2:, 1])[:, None, None] * dir_up
    )
    return (
        loss_sum / examples,
        example_norms,
        down_momentum,
        down_velocity,
        updated_down,
        up_momentum,
        up_velocity,
        updated_up,
        norm_table,
    )


def solution(mesh):
    placed = (
        P("dp", None),
        P("dp"),
        P("dp"),
        P(),
        P("dp", "head"),
        P(),
        P(None, None, "head"),
        P("head", None),
        P(None, "head"),
        P("head", None),
        P(),
        P(),
        P(),
        P(),
        P(None, None, "head"),
        P(None, "dp", None),
        P(None, "dp", None),
        P(None, None, ("head", "dp")),
        P(None, None, ("head", "dp")),
        P(None, "dp", None),
        P(None, None, ("head", "dp")),
    )
    return jax.shard_map(
        per_device,
        mesh=mesh,
        in_specs=placed,
        out_specs=(
            P(),
            P(("dp", "head")),
            P(None, "dp", None),
            P(None, "dp", None),
            P(None, "dp", None),
            P(None, None, ("head", "dp")),
            P(None, None, ("head", "dp")),
            P(None, None, ("head", "dp")),
            P(),
        ),
        check_vma=False,
    )
```

profile of v0, /device:TPU:1, one launch (start us, length us, event | category | flops | bytes accessed | tf_op | source)
XLA Modules:
  0.0 1647.0 jit_solution(5846328891770936799)
XLA Ops:
  7.3 19.8 %all_gather.9 = s32[128,512]{1,0:T(8,128)S(1)} all-gather(s32[8,512]{1,0:T(8,128)} %param.22), channel_id=1, replica_groups=mesh['dp'=16,'head'=8] {'dp'}, dimensions={0}, use_global_device_ids=true | all-gather | bytes 278528 | tf_op jit(solution)/shard_map/all_gather | solution.py:277
  28.1 229.0 %gather_fusion = bf16[65536,128]{1,0:T(8,128)(2,1)} fusion(bf16[3144,128]{1,0:T(8,128)(2,1)S(1)} %copy-done.1, s32[65536]{0:T(1024)S(1)} %broadcast_clamp_fusion), kind=kCustom, calls=%fused_computation | custom fusion | bytes 33816576 | tf_op jit(solution)/shard_map/jit(_take)/gather | solution.py:282
  257.0 46.3 %select_convert_fusion = bf16[65536,128]{1,0:T(8,128)(2,1)} fusion(bf16[65536,128]{1,0:T(8,128)(2,1)} %gather_fusion, pred[65536]{0:T(1024)(128)(4,1)S(1)} %compare_and_fusion, pred[65536]{0:T(1024)(128)(4,1)S(1)} %bitcast.555), kind=kLoop, calls=%fused_computation.1 | loop fusion | flops 33554432 | bytes 33685504 | tf_op jit(solution)/shard_map/convert_element_type | solution.py:284
  303.4 115.6 %reduce-scatter.6.cloned.1.call-done = bf16[4096,128]{1,0:T(8,128)(2,1)} async-done(((bf16[65536,128]{1,0:T(8,128)(2,1)}), bf16[4096,128]{1,0:T(8,128)(2,1)}) %reduce-scatter.6.cloned.1.call-update) | async-done | bytes 1048592 | tf_op jit(solution)/shard_map/reduce_scatter | solution.py:283
  423.8 51.6 %all-gather.2.cloned.1.call-done = bf16[4096,1024]{1,0:T(8,128)(2,1)} async-done(((bf16[4096,128]{1,0:T(8,128)(2,1)}), bf16[4096,1024]{1,0:T(8,128)(2,1)}) %all-gather.2.cloned.1.call-update) | async-done | bytes 8388624 | tf_op jit(solution)/shard_map/all_gather | solution.py:294
  480.5 5.9 multiply_reduce_fusion
  486.4 6.1 multiply_add_fusion
  580.3 183.9 %all-reduce.15.cloned.1.call-done = (f32[1024,1024]{1,0:T(8,128)}, f32[1024,1024]{1,0:T(8,128)}, f32[1024,1024]{1,0:T(8,128)}, f32[1024,1024]{1,0:T(8,128)}) async-done(((f32[1024,1024]{1,0:T(8,128)}, f32[1024,1024]{1,0:T(8,128)}, f32[1024,1024]{1,0:T(8,128)}, f32[1024,1024]{1,0:T(8,128)}), (f32[1024,1024]{1,0:T(8,128)}, f32[1024,1024]{1,0:T(8,128)}, f32[1024,1024]{1,0:T(8,128)}, ...) | async-done | bytes 16777232 | tf_op jit(solution)/shard_map/psum | solution.py:43
  777.6 6.8 fusion.140
  784.4 6.7 fusion.138
  794.9 6.7 fusion.139
  806.8 6.7 fusion.137
  814.4 183.4 %all-reduce.13.cloned.1.call-done = (f32[1024,1024]{1,0:T(8,128)}, f32[1024,1024]{1,0:T(8,128)}, f32[1024,1024]{1,0:T(8,128)}, f32[1024,1024]{1,0:T(8,128)}) async-done(((f32[1024,1024]{1,0:T(8,128)}, f32[1024,1024]{1,0:T(8,128)}, f32[1024,1024]{1,0:T(8,128)}, f32[1024,1024]{1,0:T(8,128)}), (f32[1024,1024]{1,0:T(8,128)}, f32[1024,1024]{1,0:T(8,128)}, f32[1024,1024]{1,0:T(8,128)}, ...) | async-done | bytes 16777232 | tf_op jit(solution)/shard_map/psum | solution.py:43
  997.8 12.3 fusion.371
  1019.7 5.7 fusion.24
  1027.7 8.9 fusion.18
  1036.7 10.9 fusion.144
  1051.4 11.0 fusion.143
  1062.5 7.4 fusion.29
  1069.8 10.8 fusion.142
  1080.6 10.9 fusion.141
  1102.5 173.5 %all-reduce.11.cloned.1.call-done = (f32[1024,1024]{1,0:T(8,128)}, f32[1024,1024]{1,0:T(8,128)}, f32[1024,1024]{1,0:T(8,128)}, f32[1024,1024]{1,0:T(8,128)}) async-done(((f32[1024,1024]{1,0:T(8,128)}, f32[1024,1024]{1,0:T(8,128)}, f32[1024,1024]{1,0:T(8,128)}, f32[1024,1024]{1,0:T(8,128)}), (f32[1024,1024]{1,0:T(8,128)}, f32[1024,1024]{1,0:T(8,128)}, f32[1024,1024]{1,0:T(8,128)}, ...) | async-done | bytes 16777232 | tf_op jit(solution)/shard_map/psum | solution.py:146
  1276.0 7.9 fusion.370
  1295.3 5.9 fusion.369
  1312.6 5.9 fusion.368
  1330.0 5.9 fusion.367
  1359.7 29.7 %all-reduce.16 = (bf16[1024,32]{0,1:T(8,128)(2,1)}, bf16[1024,32]{0,1:T(8,128)(2,1)}, bf16[1024,32]{0,1:T(8,128)(2,1)}, bf16[1024,32]{0,1:T(8,128)(2,1)}) all-reduce(f32[1024,32]{0,1:T(8,128)S(1)} %maximum_multiply_fusion.3, f32[1024,32]{0,1:T(8,128)} %maximum_multiply_fusion.2, ...), channel_id=1, replica_groups=mesh['dp'=16,'head'=8] {'head'}, use_global_device_ids=true, to_apply=%region_73.75 | all-reduce | flops 131072 | bytes 786432 | tf_op jit(solution)/shard_map/psum | solution.py:201
  1396.8 10.8 all_to_all.6
  1409.6 12.5 all-reduce
  1426.7 64.2 %reduce-scatter.8.cloned.1.call-done = f32[2,16,8]{1,2,0:T(8,128)} async-done(((f32[2,16,128]{1,2,0:T(8,128)}), f32[2,16,8]{1,2,0:T(8,128)}) %reduce-scatter.8.cloned.1.call-update) | async-done | bytes 1040 | tf_op jit(solution)/shard_map/reduce_scatter | solution.py:331
  1492.3 74.0 %reduce-scatter.10.cloned.1.call-done = f32[64,32]{1,0:T(8,128)} async-done(((f32[1024,32]{1,0:T(8,128)}), f32[64,32]{1,0:T(8,128)}) %reduce-scatter.10.cloned.1.call-update) | async-done | bytes 8208
  1568.7 66.1 %all-reduce.1 = (f32[]{:T(128)}, f32[2,2]{0,1:T(2,128)S(1)}, f32[2,2]{0,1:T(2,128)S(1)}) all-reduce(f32[]{:T(128)S(6)} %div.320, f32[2,2]{0,1:T(2,128)S(1)} %pad_maximum_fusion.2, f32[2,2]{0,1:T(2,128)S(1)} %maximum_multiply_fusion.8), channel_id=1, replica_groups=mesh['dp'=16,'head'=8] {'dp','head'}, use_global_device_ids=true, to_apply=%region_45.47 | all-reduce | flops 9 | bytes 72 | tf_op jit(solution)/shard_map/psum | solution.py:358
  (627 shorter events, 220.1 us)
Async XLA Ops:
  7.2 770.4 %copy-start = (bf16[512,1024]{1,0:T(8,128)(2,1)S(1)}, bf16[512,1024]{1,0:T(8,128)(2,1)}, u32[]{:S(2)}) copy-start(bf16[512,1024]{1,0:T(8,128)(2,1)} %param.31) | copy-start | bytes 3145732
  7.2 20.9 %copy-start.1 = (bf16[3144,128]{1,0:T(8,128)(2,1)S(1)}, bf16[3144,128]{1,0:T(8,128)(2,1)}, u32[]{:S(2)}) copy-start(bf16[3144,128]{1,0:T(8,128)(2,1)} %param.26) | copy-start | bytes 2414596
  7.2 411.8 %reduce-scatter.6.cloned.1.call-start = ((), (), s32[]{:S(2)}) async-start(), calls=%async_computation.4 | async-start | bytes 17825792 | tf_op jit(solution)/shard_map/reduce_scatter | solution.py:283
  303.3 172.0 %all-gather.2.cloned.1.call-start = ((), (), s32[]{:S(2)}) async-start(), calls=%async_computation.5 | async-start | bytes 9437184 | tf_op jit(solution)/shard_map/all_gather | solution.py:294
  419.0 345.2 %all-reduce.15.cloned.1.call-start = ((), (), s32[]{:S(2)}) async-start(), calls=%async_computation.10 | async-start | bytes 33554432 | tf_op jit(solution)/shard_map/psum | solution.py:43
  420.7 151.7 %copy-start.88 = (bf16[2,16,128]{2,1,0:T(8,128)(2,1)}, bf16[2,16,128]{2,1,0:T(8,128)(2,1)S(1)}, u32[]{:S(2)}) copy-start(bf16[2,16,128]{2,1,0:T(8,128)(2,1)S(1)} %convert_element_type.351) | copy-start | bytes 24580
  422.0 151.4 %copy-start.111 = (pred[2,512]{1,0:T(4,128)(4,1)}, pred[2,512]{1,0:T(4,128)(4,1)S(1)}, u32[]{:S(2)}) copy-start(pred[2,512]{1,0:T(4,128)(4,1)S(1)} %get-tuple-element.137) | copy-start | bytes 3076
  500.9 19.8 %copy-start.32 = (f32[2,512,1024]{2,1,0:T(8,128)}, f32[2,512,1024]{2,1,0:T(8,128)S(1)}, u32[]{:S(2)}) copy-start(f32[2,512,1024]{2,1,0:T(8,128)S(1)} %get-tuple-element.79) | copy-start | bytes 12582916
  523.1 14.8 copy-start.71
  524.8 8.6 copy-start.53
  542.7 15.3 copy-start.69
  544.4 9.1 copy-start.55
  580.3 417.5 %all-reduce.13.cloned.1.call-start = ((), (), s32[]{:S(2)}) async-start(), calls=%async_computation.9 | async-start | bytes 33554432 | tf_op jit(solution)/shard_map/psum | solution.py:43
  813.5 462.4 %all-reduce.11.cloned.1.call-start = ((), (), s32[]{:S(2)}) async-start(), calls=%async_computation.8 | async-start | bytes 33554432 | tf_op jit(solution)/shard_map/psum | solution.py:146
  1010.1 9.6 copy-start.2
  1010.1 9.6 copy-start.6
  1010.1 17.6 %copy-start.4 = (f32[1024,1024]{1,0:T(8,128)}, f32[1024,1024]{1,0:T(8,128)S(1)}, u32[]{:S(2)}) copy-start(f32[1024,1024]{1,0:T(8,128)S(1)} %get-tuple-element.121) | copy-start | bytes 12582916
  1010.1 17.6 %copy-start.8 = (f32[1024,1024]{1,0:T(8,128)}, f32[1024,1024]{1,0:T(8,128)S(1)}, u32[]{:S(2)}) copy-start(f32[1024,1024]{1,0:T(8,128)S(1)} %get-tuple-element.125) | copy-start | bytes 12582916
  1091.6 399.3 %reduce-scatter.8.cloned.1.call-start = ((), (), s32[]{:S(2)}) async-start(), calls=%async_computation.6 | async-start | bytes 139264 | tf_op jit(solution)/shard_map/reduce_scatter | solution.py:331
  1290.2 53.7 %copy-start.78 = (bf16[2,2,64,512]{3,2,1,0:T(8,128)(2,1)}, bf16[2,2,64,512]{3,2,1,0:T(8,128)(2,1)S(1)}, u32[]{:S(2)}) copy-start(bf16[2,2,64,512]{3,2,1,0:T(8,128)(2,1)S(1)} %convolution_convert_fusion) | copy-start | bytes 786436
  1307.6 40.5 %copy-start.80 = (bf16[2,2,64,512]{3,2,1,0:T(8,128)(2,1)}, bf16[2,2,64,512]{3,2,1,0:T(8,128)(2,1)S(1)}, u32[]{:S(2)}) copy-start(bf16[2,2,64,512]{3,2,1,0:T(8,128)(2,1)S(1)} %convolution_convert_fusion.1) | copy-start | bytes 786436
  1324.9 27.4 %copy-start.82 = (bf16[2,2,64,512]{3,2,1,0:T(8,128)(2,1)}, bf16[2,2,64,512]{3,2,1,0:T(8,128)(2,1)S(1)}, u32[]{:S(2)}) copy-start(bf16[2,2,64,512]{3,2,1,0:T(8,128)(2,1)S(1)} %convolution_convert_fusion.2) | copy-start | bytes 786436
  1342.2 13.8 copy-start.84
  1358.9 32.7 %copy-start.38 = (bf16[2,512,1024]{2,1,0:T(8,128)(2,1)S(1)}, bf16[2,512,1024]{2,1,0:T(8,128)(2,1)}, u32[]{:S(2)}) copy-start(bf16[2,512,1024]{2,1,0:T(8,128)(2,1)} %get-tuple-element.84) | copy-start | bytes 6291460
  1423.1 143.2 %reduce-scatter.10.cloned.1.call-start = ((), (), s32[]{:S(2)}) async-start(), calls=%async_computation.7 | async-start | bytes 557056
  1423.2 67.7 %copy-start.122 = (f32[2,16,8]{1,2,0:T(8,128)S(1)}, f32[2,16,8]{1,2,0:T(8,128)}, u32[]{:S(2)}) copy-start(f32[2,16,8]{1,2,0:T(8,128)} %copy.338) | copy-start | bytes 3076
  1423.2 67.7 %copy-start.153 = (f32[2,16,8]{1,2,0:T(8,128)S(1)}, f32[2,16,8]{1,2,0:T(8,128)}, u32[]{:S(2)}) copy-start(f32[2,16,8]{1,2,0:T(8,128)} %param.42) | copy-start | bytes 3076
  1423.2 67.7 %copy-start.154 = (f32[2,16,8]{1,2,0:T(8,128)S(1)}, f32[2,16,8]{1,2,0:T(8,128)}, u32[]{:S(2)}) copy-start(f32[2,16,8]{1,2,0:T(8,128)} %param.40) | copy-start | bytes 3076
  1423.2 67.7 %copy-start.155 = (f32[2,16,8]{1,2,0:T(8,128)S(1)}, f32[2,16,8]{1,2,0:T(8,128)}, u32[]{:S(2)}) copy-start(f32[2,16,8]{1,2,0:T(8,128)} %param.39) | copy-start | bytes 3076
  1424.7 142.5 %copy-start.145 = (f32[2,64,16]{1,2,0:T(8,128)S(1)}, f32[2,64,16]{1,2,0:T(8,128)}, u32[]{:S(2)}) copy-start(f32[2,64,16]{1,2,0:T(8,128)} %param.41) | copy-start | bytes 24580
  1424.7 142.5 %copy-start.146 = (f32[2,64,16]{1,2,0:T(8,128)S(1)}, f32[2,64,16]{1,2,0:T(8,128)}, u32[]{:S(2)}) copy-start(f32[2,64,16]{1,2,0:T(8,128)} %param.38) | copy-start | bytes 24580
  1424.7 142.5 %copy-start.147 = (f32[2,64,16]{1,2,0:T(8,128)S(1)}, f32[2,64,16]{1,2,0:T(8,128)}, u32[]{:S(2)}) copy-start(f32[2,64,16]{1,2,0:T(8,128)} %param.37) | copy-start | bytes 24580
  (139 other events, 371.3 us)
Sparse Core Ops, SparseCore 0:
  303.4 115.5 reduce-scatter.5
  420.7 54.6 all-gather.1
  580.4 183.7 all-reduce.14
  813.6 184.1 all-reduce.12
  1091.7 184.2 all-reduce.10
  1423.2 67.6 reduce-scatter.7
  1494.4 71.8 reduce-scatter.9
where the time goes:
time: 1650 us
  waiting for transfers between devices  846 us (51%)
  local copies, waits for them, and re-layouts  291 us (18%)
  matrix products  177 us (11%)
  other arithmetic  169 us (10%)
  blocking collectives  139 us (8%)
  between operations  24.4 us (1%)
    psum x2, waiting for transfers between devices, branch_add(): total = lax.psum(partial_out, 'head')  367 us
    gather x1, local copies, waits for them, and re-layouts, per_device(): jnp.take(token_embedding_table, jnp.clip(ids_here, 0, vocab_local - 1), a...  229 us
    psum x1, waiting for transfers between devices, layer_forward(): d_one = d_sum_two + lax.psum(back_part, 'head')  173 us
    reduce_scatter x1, waiting for transfers between devices, per_device(): lax.psum_scatter(jnp.where(inside[:, None], picked.astype(jnp.float32), 0...  116 us
    unnamed x8, waiting for transfers between devices  74.1 us
    psum x1, blocking collectives, per_device(): lax.psum((sq_down, sq_up, loss_part), ('dp', 'head'))  66.1 us
    reduce_scatter x1, waiting for transfers between devices, per_device(): lax.psum_scatter(sum_up, 'dp', scatter_dimension=2, tiled=True)  64.2 us
    all_gather x1, waiting for transfers between devices, per_device(): tokens = lax.all_gather(columns, 'head', axis=1, tiled=True)  51.6 us
  transfers between devices with their start and end apart: 7, of which 7 were waited for; matrix products, arithmetic and copies ran while one was open for 1% of the time, Pallas kernels for 0%

commit v1 on v0

--- a/solution.py
+++ b/solution.py
@@ -19,6 +19,14 @@
 contract_last = (((1,), (1,)), ((), ()))
 
 
+def doubling_sum(shard, name):
+    size, total = (lax.axis_size(name), shard)
+    for far in [1 << k for k in range(size.bit_length() - 1)]:
+        swap = [(i, i ^ far) for i in range(size)]
+        total = total + lax.ppermute(total, name, swap)
+    return total
+
+
 def gelu_exact(inputs):
     return jax.nn.gelu(inputs, approximate=False)
 
@@ -40,7 +48,7 @@
 
 
 def branch_add(partial_out, resid, gain, bias):
-    total = lax.psum(partial_out, "head")
+    total = doubling_sum(partial_out, "head")
     return norm_rows(resid + total, gain, bias)
 
 

time: 1650 us -> 2710 us (1.64)
  waiting for transfers between devices: 846 us -> 1800 us
  other arithmetic: 169 us -> 245 us
  starting transfers between devices: 0.29 us -> 30.8 us
    ppermute x0 -> x24, waiting for transfers between devices: none -> 1330 us  [doubling_sum(): total = total + lax.ppermute(total, name, swap)]
    psum x2 -> x0, waiting for transfers between devices: 367 us -> none  [branch_add(): total = lax.psum(partial_out, 'head')]
    add x0 -> x16, other arithmetic: none -> 54.2 us  [doubling_sum(): total = total + lax.ppermute(total, name, swap)]
    ppermute x0 -> x24, starting transfers between devices: none -> 30.6 us  [doubling_sum(): total = total + lax.ppermute(total, name, swap)]
    unnamed x8 -> x6, waiting for transfers between devices: 74.1 us -> 73.9 us
  transfers between devices with their start and end apart: 7 -> 29, of which waited for: 7 -> 21; matrix products, arithmetic and copies ran while one was open for 1% -> 6% of each run, Pallas kernels for 0% -> 0%
where the time goes in v1:
time: 2710 us
  waiting for transfers between devices  1800 us (66%)
  local copies, waits for them, and re-layouts  290 us (11%)
  other arithmetic  245 us (9%)
  matrix products  172 us (6%)
  blocking collectives  139 us (5%)
  starting transfers between devices  30.8 us (1%)
    ppermute x24, waiting for transfers between devices, doubling_sum(): total = total + lax.ppermute(total, name, swap)  1330 us
    gather x1, local copies, waits for them, and re-layouts, per_device(): jnp.take(token_embedding_table, jnp.clip(ids_here, 0, vocab_local - 1), a...  227 us
    psum x1, waiting for transfers between devices, layer_forward(): d_one = d_sum_two + lax.psum(back_part, 'head')  173 us
    reduce_scatter x1, waiting for transfers between devices, per_device(): lax.psum_scatter(jnp.where(inside[:, None], picked.astype(jnp.float32), 0...  116 us
    unnamed x6, waiting for transfers between devices  73.9 us
    psum x1, blocking collectives, per_device(): lax.psum((sq_down, sq_up, loss_part), ('dp', 'head'))  66.1 us
    reduce_scatter x1, waiting for transfers between devices, per_device(): lax.psum_scatter(sum_up, 'dp', scatter_dimension=2, tiled=True)  64.2 us
  transfers between devices with their start and end apart: 29, of which 21 were waited for; matrix products, arithmetic and copies ran while one was open for 6% of the time, Pallas kernels for 0%

profile of v1, /device:TPU:1, one launch (start us, length us, event | category | flops | bytes accessed | tf_op | source)
XLA Modules:
  0.0 2705.8 jit_solution(3901800284213158565)
XLA Ops:
  7.3 19.8 all_gather.9
  28.1 227.3 %gather_fusion = bf16[65536,128]{1,0:T(8,128)(2,1)} fusion(bf16[3144,128]{1,0:T(8,128)(2,1)S(1)} %copy-done.1, s32[65536]{0:T(1024)S(1)} %broadcast_clamp_fusion), kind=kCustom, calls=%fused_computation | custom fusion | bytes 33816576 | tf_op jit(solution)/shard_map/jit(_take)/gather | solution.py:290
  255.4 46.2 %select_convert_fusion = bf16[65536,128]{1,0:T(8,128)(2,1)} fusion(bf16[65536,128]{1,0:T(8,128)(2,1)} %gather_fusion, pred[65536]{0:T(1024)(128)(4,1)S(1)} %compare_and_fusion, pred[65536]{0:T(1024)(128)(4,1)S(1)} %bitcast.555), kind=kLoop, calls=%fused_computation.1 | loop fusion | flops 33554432 | bytes 33685504 | tf_op jit(solution)/shard_map/convert_element_type | solution.py:292
  301.7 115.8 %reduce-scatter.6.cloned.1.call-done = bf16[4096,128]{1,0:T(8,128)(2,1)} async-done(((bf16[65536,128]{1,0:T(8,128)(2,1)}), bf16[4096,128]{1,0:T(8,128)(2,1)}) %reduce-scatter.6.cloned.1.call-update) | async-done | bytes 1048592 | tf_op jit(solution)/shard_map/reduce_scatter | solution.py:291
  422.2 51.5 %all-gather.2.cloned.1.call-done = bf16[4096,1024]{1,0:T(8,128)(2,1)} async-done(((bf16[4096,128]{1,0:T(8,128)(2,1)}), bf16[4096,1024]{1,0:T(8,128)(2,1)}) %all-gather.2.cloned.1.call-update) | async-done | bytes 8388624 | tf_op jit(solution)/shard_map/all_gather | solution.py:302
  595.4 78.8 %collective-permute-done.19 = f32[1024,1024]{1,0:T(8,128)S(1)} collective-permute-done((f32[1024,1024]{1,0:T(8,128)S(1)}, f32[1024,1024]{1,0:T(8,128)S(1)}, u32[]{:S(2)}, u32[]{:S(2)}) %collective-permute-start.19) | collective-permute-done | bytes 4194336 | tf_op jit(solution)/shard_map/ppermute | solution.py:26
  677.6 86.6 %collective-permute-done.1 = f32[1024,1024]{1,0:T(8,128)} collective-permute-done((f32[1024,1024]{1,0:T(8,128)S(1)}, f32[1024,1024]{1,0:T(8,128)}, u32[]{:S(2)}, u32[]{:S(2)}) %collective-permute-start.1) | collective-permute-done | bytes 4194336 | tf_op jit(solution)/shard_map/ppermute | solution.py:26
  771.8 82.3 %collective-permute-done.7 = f32[1024,1024]{1,0:T(8,128)} collective-permute-done((f32[1024,1024]{1,0:T(8,128)S(1)}, f32[1024,1024]{1,0:T(8,128)}, u32[]{:S(2)}, u32[]{:S(2)}) %collective-permute-start.7) | collective-permute-done | bytes 4194336 | tf_op jit(solution)/shard_map/ppermute | solution.py:26
  859.7 84.3 %collective-permute-done.13 = f32[1024,1024]{1,0:T(8,128)} collective-permute-done((f32[1024,1024]{1,0:T(8,128)S(1)}, f32[1024,1024]{1,0:T(8,128)}, u32[]{:S(2)}, u32[]{:S(2)}) %collective-permute-start.13) | collective-permute-done | bytes 4194336 | tf_op jit(solution)/shard_map/ppermute | solution.py:26
  949.7 85.6 %collective-permute-done.20 = f32[1024,1024]{1,0:T(8,128)} collective-permute-done((f32[1024,1024]{1,0:T(8,128)S(1)}, f32[1024,1024]{1,0:T(8,128)}, u32[]{:S(2)}, u32[]{:S(2)}) %collective-permute-start.20) | collective-permute-done | bytes 4194336 | tf_op jit(solution)/shard_map/ppermute | solution.py:26
  1050.5 74.6 %collective-permute-done.2 = f32[1024,1024]{1,0:T(8,128)} collective-permute-done((f32[1024,1024]{1,0:T(8,128)}, f32[1024,1024]{1,0:T(8,128)}, u32[]{:S(2)}, u32[]{:S(2)}) %collective-permute-start.2) | collective-permute-done | bytes 4194336 | tf_op jit(solution)/shard_map/ppermute | solution.py:26
  1141.1 74.0 %collective-permute-done.8 = f32[1024,1024]{1,0:T(8,128)} collective-permute-done((f32[1024,1024]{1,0:T(8,128)S(1)}, f32[1024,1024]{1,0:T(8,128)}, u32[]{:S(2)}, u32[]{:S(2)}) %collective-permute-start.8) | collective-permute-done | bytes 4194336 | tf_op jit(solution)/shard_map/ppermute | solution.py:26
  1229.1 75.8 %collective-permute-done.14 = f32[1024,1024]{1,0:T(8,128)} collective-permute-done((f32[1024,1024]{1,0:T(8,128)S(1)}, f32[1024,1024]{1,0:T(8,128)}, u32[]{:S(2)}, u32[]{:S(2)}) %collective-permute-start.14) | collective-permute-done | bytes 4194336 | tf_op jit(solution)/shard_map/ppermute | solution.py:26
  1336.4 78.3 %collective-permute-done.22 = f32[1024,1024]{1,0:T(8,128)} collective-permute-done((f32[1024,1024]{1,0:T(8,128)S(1)}, f32[1024,1024]{1,0:T(8,128)}, u32[]{:S(2)}, u32[]{:S(2)}) %collective-permute-start.22) | collective-permute-done | bytes 4194336 | tf_op jit(solution)/shard_map/ppermute | solution.py:26
  1419.1 85.4 %collective-permute-done.4 = f32[1024,1024]{1,0:T(8,128)} collective-permute-done((f32[1024,1024]{1,0:T(8,128)S(1)}, f32[1024,1024]{1,0:T(8,128)}, u32[]{:S(2)}, u32[]{:S(2)}) %collective-permute-start.4) | collective-permute-done | bytes 4194336 | tf_op jit(solution)/shard_map/ppermute | solution.py:26
  1509.0 85.4 %collective-permute-done.10 = f32[1024,1024]{1,0:T(8,128)} collective-permute-done((f32[1024,1024]{1,0:T(8,128)S(1)}, f32[1024,1024]{1,0:T(8,128)}, u32[]{:S(2)}, u32[]{:S(2)}) %collective-permute-start.10) | collective-permute-done | bytes 4194336 | tf_op jit(solution)/shard_map/ppermute | solution.py:26
  1599.0 85.4 %collective-permute-done.16 = f32[1024,1024]{1,0:T(8,128)} collective-permute-done((f32[1024,1024]{1,0:T(8,128)S(1)}, f32[1024,1024]{1,0:T(8,128)}, u32[]{:S(2)}, u32[]{:S(2)}) %collective-permute-start.16) | collective-permute-done | bytes 4194336 | tf_op jit(solution)/shard_map/ppermute | solution.py:26
  1689.3 85.7 %collective-permute-done.23 = f32[1024,1024]{1,0:T(8,128)} collective-permute-done((f32[1024,1024]{1,0:T(8,128)S(1)}, f32[1024,1024]{1,0:T(8,128)}, u32[]{:S(2)}, u32[]{:S(2)}) %collective-permute-start.23) | collective-permute-done | bytes 4194336 | tf_op jit(solution)/shard_map/ppermute | solution.py:26
  1780.4 84.3 %collective-permute-done.5 = f32[1024,1024]{1,0:T(8,128)S(1)} collective-permute-done((f32[1024,1024]{1,0:T(8,128)S(1)}, f32[1024,1024]{1,0:T(8,128)S(1)}, u32[]{:S(2)}, u32[]{:S(2)}) %collective-permute-start.5) | collective-permute-done | bytes 4194336 | tf_op jit(solution)/shard_map/ppermute | solution.py:26
  1864.7 90.0 %collective-permute-done.11 = f32[1024,1024]{1,0:T(8,128)} collective-permute-done((f32[1024,1024]{1,0:T(8,128)S(1)}, f32[1024,1024]{1,0:T(8,128)}, u32[]{:S(2)}, u32[]{:S(2)}) %collective-permute-start.11) | collective-permute-done | bytes 4194336 | tf_op jit(solution)/shard_map/ppermute | solution.py:26
  1954.7 89.9 %collective-permute-done.17 = f32[1024,1024]{1,0:T(8,128)} collective-permute-done((f32[1024,1024]{1,0:T(8,128)S(1)}, f32[1024,1024]{1,0:T(8,128)}, u32[]{:S(2)}, u32[]{:S(2)}) %collective-permute-start.17) | collective-permute-done | bytes 4194336 | tf_op jit(solution)/shard_map/ppermute | solution.py:26
  2044.6 18.7 fusion.367
  2096.6 10.9 fusion.140
  2111.4 10.8 fusion.139
  2140.4 10.8 fusion.137
  2162.2 173.1 %all-reduce.7.cloned.1.call-done = (f32[1024,1024]{1,0:T(8,128)}, f32[1024,1024]{1,0:T(8,128)}, f32[1024,1024]{1,0:T(8,128)}, f32[1024,1024]{1,0:T(8,128)}) async-done(((f32[1024,1024]{1,0:T(8,128)}, f32[1024,1024]{1,0:T(8,128)}, f32[1024,1024]{1,0:T(8,128)}, f32[1024,1024]{1,0:T(8,128)}), (f32[1024,1024]{1,0:T(8,128)}, f32[1024,1024]{1,0:T(8,128)}, f32[1024,1024]{1,0:T(8,128)}, ...) | async-done | bytes 16777232 | tf_op jit(solution)/shard_map/psum | solution.py:154
  2419.1 29.7 %all-reduce.8 = (bf16[1024,32]{0,1:T(8,128)(2,1)}, bf16[1024,32]{0,1:T(8,128)(2,1)}, bf16[1024,32]{0,1:T(8,128)(2,1)}, bf16[1024,32]{0,1:T(8,128)(2,1)}) all-reduce(f32[1024,32]{0,1:T(8,128)S(1)} %maximum_multiply_fusion.3, f32[1024,32]{0,1:T(8,128)} %maximum_multiply_fusion.2, ...), channel_id=1, replica_groups=mesh['dp'=16,'head'=8] {'head'}, use_global_device_ids=true, to_apply=%region_65.67 | all-reduce | flops 131072 | bytes 786432 | tf_op jit(solution)/shard_map/psum | solution.py:209
  2456.1 10.8 all_to_all.6
  2469.0 12.5 all-reduce
  2486.1 64.2 %reduce-scatter.8.cloned.1.call-done = f32[2,16,8]{1,2,0:T(8,128)} async-done(((f32[2,16,128]{1,2,0:T(8,128)}), f32[2,16,8]{1,2,0:T(8,128)}) %reduce-scatter.8.cloned.1.call-update) | async-done | bytes 1040 | tf_op jit(solution)/shard_map/reduce_scatter | solution.py:339
  2551.6 73.9 %reduce-scatter.10.cloned.1.call-done = f32[64,32]{1,0:T(8,128)} async-done(((f32[1024,32]{1,0:T(8,128)}), f32[64,32]{1,0:T(8,128)}) %reduce-scatter.10.cloned.1.call-update) | async-done | bytes 8208
  2627.8 66.1 %all-reduce.1 = (f32[]{:T(128)}, f32[2,2]{0,1:T(2,128)S(1)}, f32[2,2]{0,1:T(2,128)S(1)}) all-reduce(f32[]{:T(128)S(6)} %div.320, f32[2,2]{0,1:T(2,128)S(1)} %pad_maximum_fusion.2, f32[2,2]{0,1:T(2,128)S(1)} %maximum_multiply_fusion.8), channel_id=1, replica_groups=mesh['dp'=16,'head'=8] {'dp','head'}, use_global_device_ids=true, to_apply=%region_37.39 | all-reduce | flops 9 | bytes 72 | tf_op jit(solution)/shard_map/psum | solution.py:366
  (710 shorter events, 413.4 us)
Async XLA Ops:
  7.2 1034.7 %copy-start = (bf16[512,1024]{1,0:T(8,128)(2,1)S(1)}, bf16[512,1024]{1,0:T(8,128)(2,1)}, u32[]{:S(2)}) copy-start(bf16[512,1024]{1,0:T(8,128)(2,1)} %param.31) | copy-start | bytes 3145732
  7.2 410.2 %reduce-scatter.6.cloned.1.call-start = ((), (), s32[]{:S(2)}) async-start(), calls=%async_computation.4 | async-start | bytes 17825792 | tf_op jit(solution)/shard_map/reduce_scatter | solution.py:291
  301.6 172.0 %all-gather.2.cloned.1.call-start = ((), (), s32[]{:S(2)}) async-start(), calls=%async_computation.5 | async-start | bytes 9437184 | tf_op jit(solution)/shard_map/all_gather | solution.py:302
  417.5 1917.8 %all-reduce.7.cloned.1.call-start = ((), (), s32[]{:S(2)}) async-start(), calls=%async_computation.8 | async-start | bytes 33554432 | tf_op jit(solution)/shard_map/psum | solution.py:154
  419.1 153.0 %copy-start.92 = (bf16[2,16,128]{2,1,0:T(8,128)(2,1)}, bf16[2,16,128]{2,1,0:T(8,128)(2,1)S(1)}, u32[]{:S(2)}) copy-start(bf16[2,16,128]{2,1,0:T(8,128)(2,1)S(1)} %convert_element_type.351) | copy-start | bytes 24580
  536.0 41.8 %collective-permute-start.18 = (f32[1024,1024]{1,0:T(8,128)}, f32[1024,1024]{1,0:T(8,128)}, u32[]{:S(2)}, u32[]{:S(2)}) collective-permute-start(f32[1024,1024]{1,0:T(8,128)} %fusion.400), channel_id=1, source_target_pairs={{0,1},{1,0},{2,3},{3,2},{4,5},{5,4},{6,7},{7,6},{8,9},{9,8},{10,11... | collective-permute-start | bytes 12582920 | tf_op jit(solution)/shard_map/ppermute | solution.py:26
  561.6 21.8 collective-permute-start
  571.0 17.3 collective-permute-start.6
  577.5 16.4 collective-permute-start.12
  582.2 92.0 %collective-permute-start.19 = (f32[1024,1024]{1,0:T(8,128)S(1)}, f32[1024,1024]{1,0:T(8,128)S(1)}, u32[]{:S(2)}, u32[]{:S(2)}) collective-permute-start(f32[1024,1024]{1,0:T(8,128)S(1)} %add.500), channel_id=1, source_target_pairs={{0,2},{1,3},{2,0},{3,1},{4,6},{5,7},{6,4},{7,5},{8,10},{9,11},{10,... | collective-permute-start | bytes 12582920 | tf_op jit(solution)/shard_map/ppermute | solution.py:26
  587.8 176.4 %collective-permute-start.1 = (f32[1024,1024]{1,0:T(8,128)S(1)}, f32[1024,1024]{1,0:T(8,128)}, u32[]{:S(2)}, u32[]{:S(2)}) collective-permute-start(f32[1024,1024]{1,0:T(8,128)S(1)} %add.448), channel_id=1, source_target_pairs={{0,2},{1,3},{2,0},{3,1},{4,6},{5,7},{6,4},{7,5},{8,10},{9,11},{10,... | collective-permute-start | bytes 12582920 | tf_op jit(solution)/shard_map/ppermute | solution.py:26
  592.7 261.4 %collective-permute-start.7 = (f32[1024,1024]{1,0:T(8,128)S(1)}, f32[1024,1024]{1,0:T(8,128)}, u32[]{:S(2)}, u32[]{:S(2)}) collective-permute-start(f32[1024,1024]{1,0:T(8,128)S(1)} %add.468), channel_id=1, source_target_pairs={{0,2},{1,3},{2,0},{3,1},{4,6},{5,7},{6,4},{7,5},{8,10},{9,11},{10,... | collective-permute-start | bytes 12582920 | tf_op jit(solution)/shard_map/ppermute | solution.py:26
  594.8 349.1 %collective-permute-start.13 = (f32[1024,1024]{1,0:T(8,128)S(1)}, f32[1024,1024]{1,0:T(8,128)}, u32[]{:S(2)}, u32[]{:S(2)}) collective-permute-start(f32[1024,1024]{1,0:T(8,128)S(1)} %add.484), channel_id=1, source_target_pairs={{0,2},{1,3},{2,0},{3,1},{4,6},{5,7},{6,4},{7,5},{8,10},{9,11},{10,... | collective-permute-start | bytes 12582920 | tf_op jit(solution)/shard_map/ppermute | solution.py:26
  675.1 360.1 %collective-permute-start.20 = (f32[1024,1024]{1,0:T(8,128)S(1)}, f32[1024,1024]{1,0:T(8,128)}, u32[]{:S(2)}, u32[]{:S(2)}) collective-permute-start(f32[1024,1024]{1,0:T(8,128)S(1)} %add.501), channel_id=1, source_target_pairs={{0,4},{1,5},{2,6},{3,7},{4,0},{5,1},{6,2},{7,3},{8,12},{9,13},{10,... | collective-permute-start | bytes 12582920 | tf_op jit(solution)/shard_map/ppermute | solution.py:26
  769.4 355.8 %collective-permute-start.2 = (f32[1024,1024]{1,0:T(8,128)}, f32[1024,1024]{1,0:T(8,128)}, u32[]{:S(2)}, u32[]{:S(2)}) collective-permute-start(f32[1024,1024]{1,0:T(8,128)} %add.449), channel_id=1, source_target_pairs={{0,4},{1,5},{2,6},{3,7},{4,0},{5,1},{6,2},{7,3},{8,12},{9,13},{10,... | collective-permute-start | bytes 12582920 | tf_op jit(solution)/shard_map/ppermute | solution.py:26
  857.2 357.8 %collective-permute-start.8 = (f32[1024,1024]{1,0:T(8,128)S(1)}, f32[1024,1024]{1,0:T(8,128)}, u32[]{:S(2)}, u32[]{:S(2)}) collective-permute-start(f32[1024,1024]{1,0:T(8,128)S(1)} %add.469), channel_id=1, source_target_pairs={{0,4},{1,5},{2,6},{3,7},{4,0},{5,1},{6,2},{7,3},{8,12},{9,13},{10,... | collective-permute-start | bytes 12582920 | tf_op jit(solution)/shard_map/ppermute | solution.py:26
  947.2 357.7 %collective-permute-start.14 = (f32[1024,1024]{1,0:T(8,128)S(1)}, f32[1024,1024]{1,0:T(8,128)}, u32[]{:S(2)}, u32[]{:S(2)}) collective-permute-start(f32[1024,1024]{1,0:T(8,128)S(1)} %add.485), channel_id=1, source_target_pairs={{0,4},{1,5},{2,6},{3,7},{4,0},{5,1},{6,2},{7,3},{8,12},{9,13},{10,... | collective-permute-start | bytes 12582920 | tf_op jit(solution)/shard_map/ppermute | solution.py:26
  1038.4 736.5 %copy-start.16 = (f32[1024,1024]{1,0:T(8,128)}, f32[1024,1024]{1,0:T(8,128)S(1)}, u32[]{:S(2)}) copy-start(f32[1024,1024]{1,0:T(8,128)S(1)} %get-tuple-element.69) | copy-start | bytes 12582916
  1048.6 269.3 %collective-permute-start.21 = (f32[1024,1024]{1,0:T(8,128)}, f32[1024,1024]{1,0:T(8,128)}, u32[]{:S(2)}, u32[]{:S(2)}) collective-permute-start(f32[1024,1024]{1,0:T(8,128)} %fusion.136), channel_id=1, source_target_pairs={{0,1},{1,0},{2,3},{3,2},{4,5},{5,4},{6,7},{7,6},{8,9},{9,8},{10,11... | collective-permute-start | bytes 12582920 | tf_op jit(solution)/shard_map/ppermute | solution.py:26
  1139.4 183.5 %collective-permute-start.3 = (f32[1024,1024]{1,0:T(8,128)}, f32[1024,1024]{1,0:T(8,128)}, u32[]{:S(2)}, u32[]{:S(2)}) collective-permute-start(f32[1024,1024]{1,0:T(8,128)} %fusion.133), channel_id=1, source_target_pairs={{0,1},{1,0},{2,3},{3,2},{4,5},{5,4},{6,7},{7,6},{8,9},{9,8},{10,11... | collective-permute-start | bytes 12582920 | tf_op jit(solution)/shard_map/ppermute | solution.py:26
  1226.9 101.6 %collective-permute-start.9 = (f32[1024,1024]{1,0:T(8,128)S(1)}, f32[1024,1024]{1,0:T(8,128)}, u32[]{:S(2)}, u32[]{:S(2)}) collective-permute-start(f32[1024,1024]{1,0:T(8,128)S(1)} %fusion.134), channel_id=1, source_target_pairs={{0,1},{1,0},{2,3},{3,2},{4,5},{5,4},{6,7},{7,6},{8,9},{9,8},{10,11... | collective-permute-start | bytes 12582920 | tf_op jit(solution)/shard_map/ppermute | solution.py:26
  1316.8 15.4 collective-permute-start.15
  1322.3 92.4 %collective-permute-start.22 = (f32[1024,1024]{1,0:T(8,128)S(1)}, f32[1024,1024]{1,0:T(8,128)}, u32[]{:S(2)}, u32[]{:S(2)}) collective-permute-start(f32[1024,1024]{1,0:T(8,128)S(1)} %add.506), channel_id=1, source_target_pairs={{0,2},{1,3},{2,0},{3,1},{4,6},{5,7},{6,4},{7,5},{8,10},{9,11},{10,... | collective-permute-start | bytes 12582920 | tf_op jit(solution)/shard_map/ppermute | solution.py:26
  1327.2 177.3 %collective-permute-start.4 = (f32[1024,1024]{1,0:T(8,128)S(1)}, f32[1024,1024]{1,0:T(8,128)}, u32[]{:S(2)}, u32[]{:S(2)}) collective-permute-start(f32[1024,1024]{1,0:T(8,128)S(1)} %add.456), channel_id=1, source_target_pairs={{0,2},{1,3},{2,0},{3,1},{4,6},{5,7},{6,4},{7,5},{8,10},{9,11},{10,... | collective-permute-start | bytes 12582920 | tf_op jit(solution)/shard_map/ppermute | solution.py:26
  1331.7 262.8 %collective-permute-start.10 = (f32[1024,1024]{1,0:T(8,128)S(1)}, f32[1024,1024]{1,0:T(8,128)}, u32[]{:S(2)}, u32[]{:S(2)}) collective-permute-start(f32[1024,1024]{1,0:T(8,128)S(1)} %add.474), channel_id=1, source_target_pairs={{0,2},{1,3},{2,0},{3,1},{4,6},{5,7},{6,4},{7,5},{8,10},{9,11},{10,... | collective-permute-start | bytes 12582920 | tf_op jit(solution)/shard_map/ppermute | solution.py:26
  1335.3 349.1 %collective-permute-start.16 = (f32[1024,1024]{1,0:T(8,128)S(1)}, f32[1024,1024]{1,0:T(8,128)}, u32[]{:S(2)}, u32[]{:S(2)}) collective-permute-start(f32[1024,1024]{1,0:T(8,128)S(1)} %add.490), channel_id=1, source_target_pairs={{0,2},{1,3},{2,0},{3,1},{4,6},{5,7},{6,4},{7,5},{8,10},{9,11},{10,... | collective-permute-start | bytes 12582920 | tf_op jit(solution)/shard_map/ppermute | solution.py:26
  1417.8 357.1 %collective-permute-start.23 = (f32[1024,1024]{1,0:T(8,128)S(1)}, f32[1024,1024]{1,0:T(8,128)}, u32[]{:S(2)}, u32[]{:S(2)}) collective-permute-start(f32[1024,1024]{1,0:T(8,128)S(1)} %add.507), channel_id=1, source_target_pairs={{0,4},{1,5},{2,6},{3,7},{4,0},{5,1},{6,2},{7,3},{8,12},{9,13},{10,... | collective-permute-start | bytes 12582920 | tf_op jit(solution)/shard_map/ppermute | solution.py:26
  1507.7 357.0 %collective-permute-start.5 = (f32[1024,1024]{1,0:T(8,128)S(1)}, f32[1024,1024]{1,0:T(8,128)S(1)}, u32[]{:S(2)}, u32[]{:S(2)}) collective-permute-start(f32[1024,1024]{1,0:T(8,128)S(1)} %add.457), channel_id=1, source_target_pairs={{0,4},{1,5},{2,6},{3,7},{4,0},{5,1},{6,2},{7,3},{8,12},{9,13},{10,... | collective-permute-start | bytes 12582920 | tf_op jit(solution)/shard_map/ppermute | solution.py:26
  1597.6 357.1 %collective-permute-start.11 = (f32[1024,1024]{1,0:T(8,128)S(1)}, f32[1024,1024]{1,0:T(8,128)}, u32[]{:S(2)}, u32[]{:S(2)}) collective-permute-start(f32[1024,1024]{1,0:T(8,128)S(1)} %add.475), channel_id=1, source_target_pairs={{0,4},{1,5},{2,6},{3,7},{4,0},{5,1},{6,2},{7,3},{8,12},{9,13},{10,... | collective-permute-start | bytes 12582920 | tf_op jit(solution)/shard_map/ppermute | solution.py:26
  1687.5 357.1 %collective-permute-start.17 = (f32[1024,1024]{1,0:T(8,128)S(1)}, f32[1024,1024]{1,0:T(8,128)}, u32[]{:S(2)}, u32[]{:S(2)}) collective-permute-start(f32[1024,1024]{1,0:T(8,128)S(1)} %add.491), channel_id=1, source_target_pairs={{0,4},{1,5},{2,6},{3,7},{4,0},{5,1},{6,2},{7,3},{8,12},{9,13},{10,... | collective-permute-start | bytes 12582920 | tf_op jit(solution)/shard_map/ppermute | solution.py:26
  2151.3 398.9 %reduce-scatter.8.cloned.1.call-start = ((), (), s32[]{:S(2)}) async-start(), calls=%async_computation.6 | async-start | bytes 139264 | tf_op jit(solution)/shard_map/reduce_scatter | solution.py:339
  2482.5 143.0 %reduce-scatter.10.cloned.1.call-start = ((), (), s32[]{:S(2)}) async-start(), calls=%async_computation.7 | async-start | bytes 557056
  (173 other events, 2425.6 us)
Sparse Core Ops, SparseCore 0:
  301.7 115.6 reduce-scatter.5
  419.1 54.5 all-gather.1
  2151.4 183.7 all-reduce.6
  2482.6 67.5 reduce-scatter.7
  2553.6 71.8 reduce-scatter.9
